TPU v7x, 256 devices: a whole 4x4x8 slice. The times are simulated.
256 devices in a mesh: rows: 64 (over x_hi, y, z), grp: 4 (over x_lo, core).
Axes of the slice: x: 4 (x_hi: 2, x_lo: 2; x = x_hi * 2 + x_lo), y: 4, z: 8, core: 2. Of those that a mesh axis runs over, the one named last changes fastest.
Arguments:
- table: float32 [524288, 256], P(('rows', 'grp')), may hold values from -1.5 to 1.5
- hot_slot: int32 [4096], P(('rows', 'grp')), may hold values from 0 to 2047, as said below
- cold_row: int32 [256, 256, 8], P(('rows', 'grp')), may hold values from 0 to 2047, as said below
- cold_bag: int32 [256, 256, 8], P(('rows', 'grp')), may hold values from 0 to 511
- hot_pick: int32 [65536, 8], P(('rows', 'grp')), may hold values from 0 to 4095
- dense: float32 [65536, 256], P(('rows', 'grp')), may hold values from -6 to 6
- label: int32 [65536], P(('rows', 'grp')), may hold values 0 or 1
Outputs:
- pooled: float32 [65536, 256], P(('rows', 'grp'))
- new_table: float32 [524288, 256], P(('rows', 'grp'))
- hot_new: float32 [4096, 256], replicated
Inputs may be any that keep to these rules, and one draw needn't show every extreme that they name: `hot_slot`: distinct within each device's block of 16 entries; hot row h lies in the shard of device h // 16. `cold_row`: a cold slot never names a hot row of its owner. `cold_bag`: a value of 256 or more marks an empty slot.
All inputs are finite; a program needn't handle non-finite values. No bound on the sum of `label` on one device may be relied on, other than what follows from the above.
Results may differ from a plain program's by a relative error of at most 0.0029.
Values may be sent and summed in bfloat16 or wider, within the bound.
A program may use at most 64 MiB of HBM per device.

v0:
```python
import jax
import jax.numpy as jnp
from jax import lax
from jax.sharding import PartitionSpec as P


def split_up(value, dim, peers):
    shape = value.shape
    blocks = value.reshape(*shape[:dim], peers, shape[dim] // peers, *shape[dim + 1 :])
    return jnp.moveaxis(blocks, dim, 0)


def laid_out(blocks, dim):
    blocks = jnp.moveaxis(blocks, 0, dim)
    shape = blocks.shape
    return blocks.reshape(*shape[:dim], shape[dim] * shape[dim + 1], *shape[dim + 2 :])


def exchange_both(value, axis, axes, splits, concats):
    sizes = [lax.axis_size(a) for a in axes]
    blocks = split_up(value, splits[0], sizes[0])
    blocks = jnp.moveaxis(split_up(blocks, splits[1] + 1, sizes[1]), 0, 1)
    inside = blocks.shape[2:]
    blocks = blocks.reshape(-1, *inside)
    blocks = lax.all_to_all(blocks, axis, split_axis=0, concat_axis=0, tiled=True)
    blocks = laid_out(blocks.reshape(*sizes, *inside), concats[0] + 1)
    return laid_out(blocks, concats[1])


def body(table, hot_slot, cold_row, cold_bag, hot_pick, dense, label):
    n_rows = lax.axis_size("rows")
    n_grp = lax.axis_size("grp")
    width = table.shape[1]
    samples = dense.shape[0]
    own_hot = hot_slot.shape[0]
    slots = cold_row.shape[1] * cold_row.shape[2]
    per_peer = cold_row.shape[2]
    rounded = table.astype(jnp.bfloat16)
    hot_full = lax.all_gather(table[hot_slot], ("rows", "grp"), axis=0, tiled=True)
    hot_copy = hot_full.astype(jnp.bfloat16)
    requests = cold_row[0].reshape(n_rows, n_grp, per_peer)
    arrived = exchange_both(requests, ("rows", "grp"), ("rows", "grp"), (0, 1), (0, 1))
    looked = rounded[arrived.reshape(-1)].reshape(n_rows, n_grp, per_peer, width)
    returned = lax.all_to_all(
        lax.all_to_all(looked, "rows", split_axis=0, concat_axis=0, tiled=True),
        "grp",
        split_axis=1,
        concat_axis=1,
        tiled=True,
    )
    flat_rows = returned.reshape(slots, width)
    bags = cold_bag[0].reshape(slots)
    selector = jnp.arange(samples, dtype=jnp.int32)[:, None] == bags[None, :]
    cold_pooled = jnp.dot(
        selector.astype(jnp.bfloat16), flat_rows, preferred_element_type=jnp.float32
    )
    hot_pooled = jnp.sum(hot_copy[hot_pick].astype(jnp.float32), axis=1)
    pooled = cold_pooled + hot_pooled
    score = jnp.sum(pooled * dense, axis=1) / width**0.5
    err = jax.nn.sigmoid(score) - label.astype(jnp.float32)
    grad = err[:, None] * dense
    slot_grad = lax.dot_general(
        selector.astype(jnp.float32),
        grad,
        (((0,), (0,)), ((), ())),
        precision=lax.Precision.HIGHEST,
        preferred_element_type=jnp.float32,
    )
    delivered = exchange_both(
        slot_grad.reshape(n_rows, n_grp, per_peer, width),
        ("rows", "grp"),
        ("rows", "grp"),
        (0, 1),
        (0, 1),
    )
    table_grad = jax.ops.segment_sum(
        delivered.reshape(slots, width), arrived.reshape(slots), num_segments=table.shape[0]
    )
    hot_total = hot_copy.shape[0]
    spread = jnp.repeat(grad, hot_pick.shape[1], axis=0)
    hot_local = jax.ops.segment_sum(spread, hot_pick.reshape(-1), num_segments=hot_total)
    summed = lax.psum(hot_local, ("rows", "grp"))
    start = lax.axis_index(("rows", "grp")) * own_hot
    own_grad = lax.dynamic_slice_in_dim(summed, start, own_hot, 0)
    table_grad = table_grad.at[hot_slot].add(own_grad)
    new_table = table - 0.1 * table_grad
    hot_new = hot_full - 0.1 * summed
    return (pooled, new_table, hot_new)


def solution(mesh):
    placed = (
        P(("rows", "grp"), None),
        P(("rows", "grp")),
        P(("rows", "grp"), None, None),
        P(("rows", "grp"), None, None),
        P(("rows", "grp"), None),
        P(("rows", "grp"), None),
        P(("rows", "grp")),
    )
    return jax.shard_map(
        body,
        mesh=mesh,
        in_specs=placed,
        out_specs=(P(("rows", "grp"), None), P(("rows", "grp"), None), P()),
        check_vma=False,
    )
```

profile of v0, /device:TPU:2, one launch (start us, length us, event | category | flops | bytes accessed | tf_op | source)
XLA Modules:
  0.0 783.1 jit_solution(3402326476514333365)
XLA Ops:
  8.4 2.8 gather_fusion.1
  11.2 1.5 copy.38
  12.7 14.7 %all-to-all-start = ((s32[256,1,1,8]{3,2,1,0:T(1,128)}), s32[256,1,1,8]{3,2,1,0:T(1,128)S(1)}, u32[]{:S(2)}, u32[]{:S(2)}) async-start(s32[256,1,1,8]{3,2,1,0:T(1,128)} %bitcast), calls=%async_computation | async-start | bytes 262144 | tf_op jit(solution)/shard_map/all_to_all | solution.py:25
  27.4 1.7 convert_element_type.14
  29.1 10.6 %all-to-all-done = s32[256,1,1,8]{3,2,1,0:T(1,128)S(1)} async-done(((s32[256,1,1,8]{3,2,1,0:T(1,128)}), s32[256,1,1,8]{3,2,1,0:T(1,128)S(1)}, u32[]{:S(2)}, u32[]{:S(2)}) %all-to-all-start) | async-done | bytes 8224 | tf_op jit(solution)/shard_map/all_to_all | solution.py:25
  39.8 7.5 gather_fusion
  47.3 34.3 %all_to_all.20 = bf16[64,4,8,256]{3,2,1,0:T(8,128)(2,1)S(1)} all-to-all(bf16[64,4,8,256]{3,2,1,0:T(8,128)(2,1)S(1)} %bitcast.38), channel_id=1, replica_groups=mesh['rows'=64,'grp'=4] {'rows'}, dimensions={0} | all-to-all | bytes 2097152 | tf_op jit(solution)/shard_map/all_to_all | solution.py:45
  81.6 1.0 copy.39
  82.6 4.7 all-to-all-start.2
  88.7 12.2 %all-to-all-done.2 = bf16[64,4,8,256]{3,2,0,1:T(8,128)(2,1)S(1)} async-done(((bf16[64,4,8,256]{3,2,0,1:T(8,128)(2,1)}), bf16[64,4,8,256]{3,2,0,1:T(8,128)(2,1)S(1)}, u32[]{:S(2)}, u32[]{:S(2)}) %all-to-all-start.2) | async-done | bytes 1048608 | tf_op jit(solution)/shard_map/all_to_all | solution.py:44
  100.9 1.1 copy.40
  102.0 330.1 %all-gather.3.cloned.1.call-done = f32[4096,256]{1,0:T(8,128)} async-done(((f32[16,256]{1,0:T(8,128)}), f32[4096,256]{1,0:T(8,128)}) %all-gather.3.cloned.1.call-update) | async-done | bytes 4194320 | tf_op jit(solution)/shard_map/all_gather | solution.py:39
  432.1 2.4 convert_element_type.15
  434.5 7.5 gather_fusion.2
  442.9 2.0 multiply_reduce_fusion
  445.0 3.2 fusion.7
  448.2 9.4 %all-to-all-start.3 = ((f32[256,1,1,8,256]{4,3,2,1,0:T(8,128)}), f32[256,1,1,8,256]{4,3,2,1,0:T(8,128)S(1)}, u32[]{:S(2)}, u32[]{:S(2)}) async-start(f32[256,1,1,8,256]{4,3,2,1,0:T(8,128)} %fusion.7), calls=%async_computation.3 | async-start | bytes 4194304 | tf_op jit(solution)/shard_map/all_to_all | solution.py:25
  458.0 13.8 %scatter_custom_fusion.1 = f32[4096,256]{1,0:T(8,128)} fusion(s32[2048]{0:T(1024)S(1)} %reshape.98, f32[]{:T(128)} %constant.15.clone.1, f32[256,256]{1,0:T(8,128)S(1)} %broadcast_multiply_fusion), kind=kCustom, calls=%fused_computation.10 | custom fusion | flops 524288 | bytes 4456452 | tf_op jit(solution)/shard_map/scatter-add | solution.py:81
  472.0 0.8 copy.46
  472.9 277.2 %all-reduce.2.cloned.1.call-done = f32[4096,256]{1,0:T(8,128)} async-done(((f32[4096,256]{1,0:T(8,128)}), f32[4096,256]{1,0:T(8,128)}) %all-reduce.2.cloned.1.call-update) | async-done | bytes 4194320 | tf_op jit(solution)/shard_map/psum | solution.py:82
  750.1 6.0 multiply_subtract_fusion
  756.1 13.0 %scatter_custom_fusion = f32[2048,256]{1,0:T(8,128)} fusion(s32[2048]{0:T(1024)S(1)} %reshape.90, f32[256,1,1,8,256]{4,3,2,1,0:T(8,128)S(1)} %all-to-all-done.3, f32[]{:T(128)} %constant.15.clone.1), kind=kCustom, calls=%fused_computation.7 | custom fusion | flops 524288 | bytes 4194308 | tf_op jit(solution)/shard_map/scatter-add | solution.py:76
  769.2 3.9 scatter_custom_fusion.2
  773.0 3.2 multiply_subtract_fusion.1
  (38 shorter events, 4.3 us)
Async XLA Ops:
  7.2 425.0 %all-gather.3.cloned.1.call-start = ((), (), s32[]{:S(2)}) async-start(), calls=%async_computation.5 | async-start | bytes 4210688 | tf_op jit(solution)/shard_map/all_gather | solution.py:39
  7.9 0.5 copy-start.6
  12.7 27.0 %all-to-all-start = ((s32[256,1,1,8]{3,2,1,0:T(1,128)}), s32[256,1,1,8]{3,2,1,0:T(1,128)S(1)}, u32[]{:S(2)}, u32[]{:S(2)}) async-start(s32[256,1,1,8]{3,2,1,0:T(1,128)} %bitcast), calls=%async_computation | async-start | bytes 262144 | tf_op jit(solution)/shard_map/all_to_all | solution.py:25
  81.6 5.7 copy-start.1
  81.6 6.6 copy-start.2
  81.6 6.8 copy-start.4
  82.6 18.3 %all-to-all-start.2 = ((bf16[64,4,8,256]{3,2,0,1:T(8,128)(2,1)}), bf16[64,4,8,256]{3,2,0,1:T(8,128)(2,1)S(1)}, u32[]{:S(2)}, u32[]{:S(2)}) async-start(bf16[64,4,8,256]{3,2,0,1:T(8,128)(2,1)} %copy.39), calls=%async_computation.2 | async-start | bytes 2097152 | tf_op jit(solution)/shard_map/all_to_all | solution.py:44
  442.0 2.8 copy-start.5
  448.2 9.6 %copy-start.3 = (s32[256,8]{0,1:T(8,128)S(1)}, s32[256,8]{0,1:T(8,128)}, u32[]{:S(2)}) copy-start(s32[256,8]{0,1:T(8,128)} %param.11) | copy-start | bytes 24580
  448.2 308.0 %all-to-all-start.3 = ((f32[256,1,1,8,256]{4,3,2,1,0:T(8,128)}), f32[256,1,1,8,256]{4,3,2,1,0:T(8,128)S(1)}, u32[]{:S(2)}, u32[]{:S(2)}) async-start(f32[256,1,1,8,256]{4,3,2,1,0:T(8,128)} %fusion.7), calls=%async_computation.3 | async-start | bytes 4194304 | tf_op jit(solution)/shard_map/all_to_all | solution.py:25
  457.5 292.6 %all-reduce.2.cloned.1.call-start = ((), (), s32[]{:S(2)}) async-start(), calls=%async_computation.4 | async-start | bytes 8388608 | tf_op jit(solution)/shard_map/psum | solution.py:82
  769.2 3.9 copy-start
Sparse Core Ops, SparseCore 0:
  11.3 420.7 all-gather.2
  472.0 278.0 all-reduce.1
where the time goes:
time: 784 us; the launch traced here: 783 us
  waiting for transfers between devices  630 us (80%)
  other arithmetic  45.5 us (6%)
  blocking collectives  34.3 us (4%)
  starting transfers between devices  29 us (4%)
  local copies, waits for them, and re-layouts  24.8 us (3%)
  between operations  14.2 us (2%)
    all_gather x1, waiting for transfers between devices, body(): lax.all_gather(table[hot_slot], ('rows', 'grp'), axis=0, tiled=True)  330 us
    psum x1, waiting for transfers between devices, body(): summed = lax.psum(hot_local, ('rows', 'grp'))  277 us
    all_to_all x1, blocking collectives, body(): lax.all_to_all(looked, 'rows', split_axis=0, concat_axis=0, tiled=True)  34.3 us
    all_to_all x2, starting transfers between devices, exchange_both(): lax.all_to_all(blocks, axis, split_axis=0, concat_axis=0, tiled=True)  24 us
  transfers between devices with their start and end apart: 5, of which 4 were waited for; matrix products, arithmetic and copies ran while one was open for 5% of the time, Pallas kernels for 0%

commit v1 on v0

--- a/solution.py
+++ b/solution.py
@@ -36,7 +36,12 @@
     slots = cold_row.shape[1] * cold_row.shape[2]
     per_peer = cold_row.shape[2]
     rounded = table.astype(jnp.bfloat16)
-    hot_full = lax.all_gather(table[hot_slot], ("rows", "grp"), axis=0, tiled=True)
+    hot_full = jnp.concatenate(
+        lax.all_to_all(
+            jnp.stack([table[hot_slot]] * lax.axis_size(("rows", "grp"))), ("rows", "grp"), 0, 0
+        ),
+        axis=0,
+    )
     hot_copy = hot_full.astype(jnp.bfloat16)
     requests = cold_row[0].reshape(n_rows, n_grp, per_peer)
     arrived = exchange_both(requests, ("rows", "grp"), ("rows", "grp"), (0, 1), (0, 1))

time: 784 us -> 554 us (0.71)
  waiting for transfers between devices: 630 us -> 391 us
  starting transfers between devices: 29 us -> 36.9 us
    all_gather x1 -> x0, waiting for transfers between devices: 330 us -> none  [body(): lax.all_gather(table[hot_slot], ('rows', 'grp'), axis=0, tiled=True)]
    all_to_all x0 -> x1, waiting for transfers between devices: none -> 93 us  [body(): lax.all_to_all(jnp.stack([table[hot_slot]] * lax.axis_size(('rows', 'grp'...]
    all_to_all x0 -> x1, starting transfers between devices: none -> 9.22 us  [body(): lax.all_to_all(jnp.stack([table[hot_slot]] * lax.axis_size(('rows', 'grp'...]
where the time goes in v1:
time: 554 us; the launch traced here: 553 us
  waiting for transfers between devices  391 us (71%)
  other arithmetic  44.8 us (8%)
  starting transfers between devices  36.9 us (7%)
  blocking collectives  34.3 us (6%)
  local copies, waits for them, and re-layouts  26.7 us (5%)
  between operations  14.2 us (3%)
    psum x1, waiting for transfers between devices, body(): summed = lax.psum(hot_local, ('rows', 'grp'))  277 us
    all_to_all x1, waiting for transfers between devices, body(): lax.all_to_all(jnp.stack([table[hot_slot]] * lax.axis_size(('rows', 'grp'...  93 us
    all_to_all x1, blocking collectives, body(): lax.all_to_all(looked, 'rows', split_axis=0, concat_axis=0, tiled=True)  34.3 us
    all_to_all x2, starting transfers between devices, exchange_both(): lax.all_to_all(blocks, axis, split_axis=0, concat_axis=0, tiled=True)  22.7 us
    scatter-add x1, other arithmetic, body(): jax.ops.segment_sum(spread, hot_pick.reshape(-1), num_segments=hot_total)  13.8 us
    scatter-add x1, other arithmetic, body(): jax.ops.segment_sum(delivered.reshape(slots, width), arrived.reshape(slot...  13 us
  transfers between devices with their start and end apart: 5, of which 4 were waited for; matrix products, arithmetic and copies ran while one was open for 5% of the time, Pallas kernels for 0%

profile of v1, /device:TPU:2, one launch (start us, length us, event | category | flops | bytes accessed | tf_op | source)
XLA Modules:
  0.0 553.0 jit_solution(8040631235972596761)
XLA Ops:
  7.2 1.5 copy.38
  8.7 14.7 %all-to-all-start = ((s32[256,1,1,8]{3,2,1,0:T(1,128)}), s32[256,1,1,8]{3,2,1,0:T(1,128)S(1)}, u32[]{:S(2)}, u32[]{:S(2)}) async-start(s32[256,1,1,8]{3,2,1,0:T(1,128)} %bitcast), calls=%async_computation | async-start | bytes 262144 | tf_op jit(solution)/shard_map/all_to_all | solution.py:25
  23.3 1.7 convert_element_type.14
  25.0 10.6 %all-to-all-done = s32[256,1,1,8]{3,2,1,0:T(1,128)S(1)} async-done(((s32[256,1,1,8]{3,2,1,0:T(1,128)}), s32[256,1,1,8]{3,2,1,0:T(1,128)S(1)}, u32[]{:S(2)}, u32[]{:S(2)}) %all-to-all-start) | async-done | bytes 8224 | tf_op jit(solution)/shard_map/all_to_all | solution.py:25
  35.8 7.5 %gather_fusion = bf16[2048,256]{1,0:T(8,128)(2,1)S(1)} fusion(bf16[2048,256]{1,0:T(8,128)(2,1)S(1)} %convert_element_type.14, s32[2048]{0:T(1024)S(1)} %broadcast_clamp_fusion.1), kind=kCustom, calls=%fused_computation | custom fusion | bytes 2105344 | tf_op jit(solution)/shard_map/gather | solution.py:48
  43.3 34.3 %all_to_all.25 = bf16[64,4,8,256]{3,2,1,0:T(8,128)(2,1)S(1)} all-to-all(bf16[64,4,8,256]{3,2,1,0:T(8,128)(2,1)S(1)} %bitcast.41), channel_id=1, replica_groups=mesh['rows'=64,'grp'=4] {'rows'}, dimensions={0} | all-to-all | bytes 2097152 | tf_op jit(solution)/shard_map/all_to_all | solution.py:50
  78.6 4.7 all-to-all-start.2
  83.9 2.2 gather_fusion.1
  86.0 10.1 %all-to-all-done.2 = bf16[64,4,8,256]{3,2,0,1:T(8,128)(2,1)S(1)} async-done(((bf16[64,4,8,256]{3,2,0,1:T(8,128)(2,1)}), bf16[64,4,8,256]{3,2,0,1:T(8,128)(2,1)S(1)}, u32[]{:S(2)}, u32[]{:S(2)}) %all-to-all-start.2) | async-done | bytes 1048608 | tf_op jit(solution)/shard_map/all_to_all | solution.py:49
  96.1 2.5 stack.2
  98.7 9.2 %all-to-all-start.3 = ((f32[256,16,256]{2,1,0:T(8,128)}), f32[256,16,256]{2,1,0:T(8,128)}, u32[]{:S(2)}, u32[]{:S(2)}) async-start(f32[256,16,256]{2,1,0:T(8,128)} %stack.2), calls=%async_computation.3 | async-start | bytes 8388608 | tf_op jit(solution)/shard_map/all_to_all | solution.py:40
  109.3 1.1 copy.40
  110.4 93.0 %all-to-all-done.3 = f32[256,16,256]{2,1,0:T(8,128)} async-done(((f32[256,16,256]{2,1,0:T(8,128)}), f32[256,16,256]{2,1,0:T(8,128)}, u32[]{:S(2)}, u32[]{:S(2)}) %all-to-all-start.3) | async-done | bytes 4194336 | tf_op jit(solution)/shard_map/all_to_all | solution.py:40
  203.4 2.4 bitcast_convert_fusion
  205.8 7.5 %gather_fusion.2 = bf16[2048,256]{1,0:T(8,128)(2,1)S(1)} fusion(bf16[4096,256]{1,0:T(8,128)(2,1)S(1)} %bitcast_convert_fusion, s32[2048]{0:T(1024)S(1)} %broadcast_clamp_fusion), kind=kCustom, calls=%fused_computation.2 | custom fusion | bytes 2105344 | tf_op jit(solution)/shard_map/gather | solution.py:62
  214.1 2.0 multiply_reduce_fusion
  216.3 3.2 fusion.7
  219.4 8.1 %all-to-all-start.4 = ((f32[256,1,1,8,256]{4,3,2,1,0:T(8,128)}), f32[256,1,1,8,256]{4,3,2,1,0:T(8,128)S(1)}, u32[]{:S(2)}, u32[]{:S(2)}) async-start(f32[256,1,1,8,256]{4,3,2,1,0:T(8,128)} %fusion.7), calls=%async_computation.4 | async-start | bytes 4194304 | tf_op jit(solution)/shard_map/all_to_all | solution.py:25
  228.0 13.8 %scatter_custom_fusion.1 = f32[4096,256]{1,0:T(8,128)} fusion(s32[2048]{0:T(1024)S(1)} %reshape.104, f32[]{:T(128)} %constant.15.clone.1, f32[256,256]{1,0:T(8,128)S(1)} %broadcast_multiply_fusion), kind=kCustom, calls=%fused_computation.11 | custom fusion | flops 524288 | bytes 4456452 | tf_op jit(solution)/shard_map/scatter-add | solution.py:86
  242.8 277.2 %all-reduce.2.cloned.1.call-done = f32[4096,256]{1,0:T(8,128)} async-done(((f32[4096,256]{1,0:T(8,128)}), f32[4096,256]{1,0:T(8,128)}) %all-reduce.2.cloned.1.call-update) | async-done | bytes 4194320 | tf_op jit(solution)/shard_map/psum | solution.py:87
  520.1 6.0 %bitcast_subtract_fusion = f32[4096,256]{1,0:T(8,128)} fusion(f32[256,16,256]{2,1,0:T(8,128)} %all-to-all-done.3, f32[4096,256]{1,0:T(8,128)} %all-reduce.2.cloned.1.call-done), kind=kLoop, calls=%fused_computation.6 | loop fusion | flops 2097152 | bytes 12582912 | tf_op jit(solution)/shard_map/sub | solution.py:92
  526.1 13.0 %scatter_custom_fusion = f32[2048,256]{1,0:T(8,128)} fusion(s32[2048]{0:T(1024)S(1)} %reshape.96, f32[256,1,1,8,256]{4,3,2,1,0:T(8,128)S(1)} %all-to-all-done.4, f32[]{:T(128)} %constant.15.clone.1), kind=kCustom, calls=%fused_computation.8 | custom fusion | flops 524288 | bytes 4194308 | tf_op jit(solution)/shard_map/scatter-add | solution.py:81
  539.1 3.9 scatter_custom_fusion.2
  543.0 3.2 multiply_subtract_fusion
  (40 shorter events, 5.5 us)
Async XLA Ops:
  8.7 27.0 %all-to-all-start = ((s32[256,1,1,8]{3,2,1,0:T(1,128)}), s32[256,1,1,8]{3,2,1,0:T(1,128)S(1)}, u32[]{:S(2)}, u32[]{:S(2)}) async-start(s32[256,1,1,8]{3,2,1,0:T(1,128)} %bitcast), calls=%async_computation | async-start | bytes 262144 | tf_op jit(solution)/shard_map/all_to_all | solution.py:25
  77.6 5.7 %copy-start.7 = (s32[16]{0:T(128)S(1)}, s32[16]{0:T(128)}, u32[]{:S(2)}) copy-start(s32[16]{0:T(128)} %param.8) | copy-start | bytes 196
  78.6 17.5 %all-to-all-start.2 = ((bf16[64,4,8,256]{3,2,0,1:T(8,128)(2,1)}), bf16[64,4,8,256]{3,2,0,1:T(8,128)(2,1)S(1)}, u32[]{:S(2)}, u32[]{:S(2)}) async-start(bf16[64,4,8,256]{3,2,0,1:T(8,128)(2,1)} %copy.39), calls=%async_computation.2 | async-start | bytes 2097152 | tf_op jit(solution)/shard_map/all_to_all | solution.py:49
  83.3 0.5 copy-start.6
  98.7 9.2 %copy-start.1 = (f32[256,256]{1,0:T(8,128)S(1)}, f32[256,256]{1,0:T(8,128)}, u32[]{:S(2)}) copy-start(f32[256,256]{1,0:T(8,128)} %param.12) | copy-start | bytes 786436
  98.7 10.1 %copy-start.2 = (s32[256,8]{0,1:T(8,128)S(1)}, s32[256,8]{0,1:T(8,128)}, u32[]{:S(2)}) copy-start(s32[256,8]{0,1:T(8,128)} %param.11) | copy-start | bytes 24580
  98.7 10.3 %copy-start.4 = (s32[1,256,8]{1,2,0:T(8,128)S(1)}, s32[1,256,8]{1,2,0:T(8,128)}, u32[]{:S(2)}) copy-start(s32[1,256,8]{1,2,0:T(8,128)} %param.10) | copy-start | bytes 24580
  98.7 104.7 %all-to-all-start.3 = ((f32[256,16,256]{2,1,0:T(8,128)}), f32[256,16,256]{2,1,0:T(8,128)}, u32[]{:S(2)}, u32[]{:S(2)}) async-start(f32[256,16,256]{2,1,0:T(8,128)} %stack.2), calls=%async_computation.3 | async-start | bytes 8388608 | tf_op jit(solution)/shard_map/all_to_all | solution.py:40
  213.3 2.8 copy-start.5
  219.4 8.3 %copy-start.3 = (s32[256,8]{0,1:T(8,128)S(1)}, s32[256,8]{0,1:T(8,128)}, u32[]{:S(2)}) copy-start(s32[256,8]{0,1:T(8,128)} %param.11) | copy-start | bytes 24580
  219.4 306.7 %all-to-all-start.4 = ((f32[256,1,1,8,256]{4,3,2,1,0:T(8,128)}), f32[256,1,1,8,256]{4,3,2,1,0:T(8,128)S(1)}, u32[]{:S(2)}, u32[]{:S(2)}) async-start(f32[256,1,1,8,256]{4,3,2,1,0:T(8,128)} %fusion.7), calls=%async_computation.4 | async-start | bytes 4194304 | tf_op jit(solution)/shard_map/all_to_all | solution.py:25
  227.5 292.6 %all-reduce.2.cloned.1.call-start = ((), (), s32[]{:S(2)}) async-start(), calls=%async_computation.5 | async-start | bytes 8388608 | tf_op jit(solution)/shard_map/psum | solution.py:87
  539.1 3.9 copy-start
Sparse Core Ops, SparseCore 0:
  242.0 278.0 all-reduce.1
